TPU v7x, 256 devices: a whole 4x4x8 slice. The times are simulated.
256 devices in a mesh: seq: 16 (over x, y), head: 16 (over z, core).
Axes of the slice: x: 4, y: 4, z: 8, core: 2. Of those that a mesh axis runs over, the one named last changes fastest.
Arguments:
- layer_input: bfloat16 [8192, 4096], P('seq', 'head'), may hold values from -40 to 40
- qk_weight: bfloat16 [4096, 4096], P('seq', 'head'), may hold values from -0.09375 to 0.09375
- value_weight: bfloat16 [4096, 4096], P('seq', 'head'), may hold values from -0.09375 to 0.09375
- groups: int32 [2, 8192, 1], P(None, 'seq'), may hold values from 0 to 15; in each aligned block of 512 rows (0 to 511, 512 to 1023, ..., all dimensions but the last counted through in order) at most 48 rows name the same one
- buckets: int32 [2, 8192], P(None, 'seq'), may hold values from 0 to 7
- out_cotangent: bfloat16 [8192, 4096], P('seq', 'head'), may hold values from -6 to 6
Outputs:
- output: bfloat16 [8192, 4096], P('seq', 'head')
- input_grad: bfloat16 [8192, 4096], P('seq', 'head')
- qk_weight_grad: float32 [4096, 4096], P('seq', 'head')
- value_weight_grad: float32 [4096, 4096], P('seq', 'head')
Inputs may be any that keep to these rules, and one draw needn't show every extreme that they name: `groups`: among the 512 tokens of one device in one round no group is named more than 48 times, and in every draw some device's tokens name some group exactly 48 times.
All inputs are finite; a program needn't handle non-finite values.
Results may differ from a plain program's by a relative error of at most 0.018.
The roundings to bfloat16 on the way count: a program that leaves them out, or rounds other values in their place, can miss the bound.
Values may be sent and summed in bfloat16 or wider, within the bound.
A program may use at most 128 MiB of HBM per device.

v0:
```python
import math
import jax
import jax.numpy as jnp
from jax import lax
from jax.sharding import PartitionSpec as P

HEAD_DIM = 128
ROUNDS = 2
BLOCK_LEN = 128
SUB_BUCKETS = 8
EPSILON = 1e-06
SELF_SCORE = -100000.0
MASKED_SCORE = -1000000000.0


def key_factor(query_f):
    return lax.rsqrt(jnp.mean(query_f * query_f, axis=-1, keepdims=True) + EPSILON) / math.sqrt(
        query_f.shape[-1]
    )


def with_previous(blocked):
    return jnp.concatenate([blocked, jnp.roll(blocked, 1, axis=0)], axis=1)


def fold_previous(block_grads, block_width):
    return block_grads[:, :block_width] + jnp.roll(block_grads[:, block_width:], -1, axis=0)


def attention_rows(queries, values, live_slots):
    slot_total, heads_here, head_width = queries.shape
    blocks = slot_total // BLOCK_LEN
    query_f = queries.astype(jnp.float32)
    factor = key_factor(query_f)
    normed = (query_f * factor).astype(jnp.bfloat16)
    query_blocks = queries.reshape(blocks, BLOCK_LEN, heads_here, head_width)
    key_blocks = with_previous(normed.reshape(blocks, BLOCK_LEN, heads_here, head_width))
    value_blocks = with_previous(values.reshape(blocks, BLOCK_LEN, heads_here, head_width))
    live_keys = with_previous(live_slots.reshape(blocks, BLOCK_LEN))
    self_pairs = jnp.arange(BLOCK_LEN)[:, None] == jnp.arange(2 * BLOCK_LEN)[None, :]
    scores = jnp.einsum(
        "nqhd,nkhd->nhqk", query_blocks, key_blocks, preferred_element_type=jnp.float32
    )
    scores = jnp.where(self_pairs, SELF_SCORE, scores)
    scores = jnp.where(live_keys[:, None, None, :], scores, MASKED_SCORE)
    largest = jnp.max(scores, axis=-1, keepdims=True)
    exponent = jnp.exp(scores - largest)
    row_total = jnp.sum(exponent, axis=-1, keepdims=True)
    weights = exponent / row_total
    log_total = (largest + jnp.log(row_total))[..., 0]
    return (weights, log_total, query_blocks, key_blocks, value_blocks, self_pairs, factor)


def forward_rows(queries, values, live_slots):
    slot_total, heads_here, head_width = queries.shape
    weights, log_total, query_blocks, key_blocks, value_blocks, self_pairs, factor = attention_rows(
        queries, values, live_slots
    )
    mixed_rows = jnp.einsum(
        "nhqk,nkhd->nqhd",
        weights.astype(jnp.bfloat16),
        value_blocks,
        preferred_element_type=jnp.float32,
    )
    return (
        mixed_rows.reshape(slot_total, heads_here, head_width),
        jnp.transpose(log_total, (0, 2, 1)).reshape(slot_total, heads_here),
    )


def backward_rows(queries, values, live_slots, out_grads, mixes, inners):
    slot_total, heads_here, head_width = queries.shape
    blocks = slot_total // BLOCK_LEN
    weights, log_total, query_blocks, key_blocks, value_blocks, self_pairs, factor = attention_rows(
        queries, values, live_slots
    )
    mix_blocks = jnp.transpose(mixes.reshape(blocks, BLOCK_LEN, heads_here), (0, 2, 1))[..., None]
    inner_blocks = jnp.transpose(inners.reshape(blocks, BLOCK_LEN, heads_here), (0, 2, 1))[
        ..., None
    ]
    scaled = (weights * mix_blocks).astype(jnp.bfloat16)
    grad_blocks = out_grads.reshape(blocks, BLOCK_LEN, heads_here, head_width)
    value_grads = fold_previous(
        jnp.einsum("nhqk,nqhd->nkhd", scaled, grad_blocks, preferred_element_type=jnp.float32),
        BLOCK_LEN,
    )
    pair_grads = jnp.einsum(
        "nqhd,nkhd->nhqk", grad_blocks, value_blocks, preferred_element_type=jnp.float32
    )
    score_grads = jnp.where(
        self_pairs, 0.0, weights * mix_blocks * (pair_grads - inner_blocks)
    ).astype(jnp.bfloat16)
    query_part = jnp.einsum(
        "nhqk,nkhd->nqhd", score_grads, key_blocks, preferred_element_type=jnp.float32
    ).reshape(slot_total, heads_here, head_width)
    key_part = fold_previous(
        jnp.einsum(
            "nhqk,nqhd->nkhd", score_grads, query_blocks, preferred_element_type=jnp.float32
        ),
        BLOCK_LEN,
    ).reshape(slot_total, heads_here, head_width)
    query_f = queries.astype(jnp.float32)
    result = (
        query_part
        + factor * key_part
        - factor * factor * factor * jnp.sum(key_part * query_f, axis=-1, keepdims=True) * query_f
    )
    return (
        result.astype(jnp.bfloat16),
        value_grads.reshape(slot_total, heads_here, head_width).astype(jnp.bfloat16),
    )


def spread_rows(token_rows, source_rows):
    padded = jnp.concatenate(
        [token_rows, jnp.zeros((1,) + token_rows.shape[1:], token_rows.dtype)], axis=0
    )
    return padded[source_rows]


def per_device(layer_input, qk_weight, value_weight, groups, buckets, out_cotangent):
    tokens_here = layer_input.shape[0]
    width_here = layer_input.shape[1]
    heads_here = width_here // HEAD_DIM
    seq_count = lax.axis_size("seq")
    token_total = tokens_here * seq_count
    capacity = 3 * tokens_here // (2 * seq_count)
    slot_count = seq_count * capacity
    features = lax.all_gather(layer_input, "head", axis=1, tiled=True)
    stacked = jnp.stack((qk_weight, value_weight))
    full_weights = lax.all_gather(stacked, "seq", axis=1, tiled=True)
    projected = jnp.einsum(
        "td,kdc->tkc", features, full_weights, preferred_element_type=jnp.float32
    )
    queries = projected[:, 0].astype(jnp.bfloat16).reshape(tokens_here, heads_here, HEAD_DIM)
    values = projected[:, 1].astype(jnp.bfloat16).reshape(tokens_here, heads_here, HEAD_DIM)
    position = lax.axis_index("seq") * tokens_here + jnp.arange(tokens_here, dtype=jnp.int32)
    sentinel = SUB_BUCKETS * token_total
    source_list = []
    slot_list = []
    key_list = []
    for turn_index in range(ROUNDS):
        target = groups[turn_index, :, 0]
        one_hot = (target[:, None] == jnp.arange(seq_count, dtype=jnp.int32)[None, :]).astype(
            jnp.int32
        )
        dest_rank = jnp.sum(jnp.cumsum(one_hot, axis=0) * one_hot, axis=1) - 1
        slot_index = target * capacity + dest_rank
        source_list.append(
            jnp.full((slot_count,), tokens_here, jnp.int32)
            .at[slot_index]
            .set(jnp.arange(tokens_here, dtype=jnp.int32))
        )
        slot_list.append(slot_index)
        sort_keys = (
            jnp.full((slot_count,), sentinel, jnp.int32)
            .at[slot_index]
            .set(buckets[turn_index] * token_total + position)
        )
        key_list.append(sort_keys.reshape(seq_count, capacity))
    arrived_keys = lax.all_to_all(
        jnp.stack(key_list, axis=1), "seq", split_axis=0, concat_axis=0, tiled=True
    )
    orderings = []
    inverses = []
    live_list = []
    for turn_index in range(ROUNDS):
        received = arrived_keys[:, turn_index].reshape(slot_count)
        ordering = jnp.argsort(received, stable=True)
        orderings.append(ordering)
        inverses.append(jnp.argsort(ordering))
        live_list.append(received[ordering] < sentinel)

    def pack_rows(token_rows):
        return jnp.stack(
            [
                spread_rows(token_rows, source_list[turn_index]).reshape(
                    (seq_count, capacity) + token_rows.shape[1:]
                )
                for turn_index in range(ROUNDS)
            ],
            axis=1,
        )

    def sorted_rows(buffer, turn_index):
        return buffer[:, turn_index].reshape((slot_count,) + buffer.shape[3:])[
            orderings[turn_index]
        ]

    def unsorted(token_rows, turn_index):
        return token_rows[inverses[turn_index]].reshape(
            (seq_count, capacity) + token_rows.shape[1:]
        )

    def home_rows(buffer, turn_index):
        return buffer[:, turn_index].reshape((slot_count,) + buffer.shape[3:])[
            slot_list[turn_index]
        ]

    query_buffer = pack_rows(queries)
    value_buffer = pack_rows(values)
    got_queries, got_values = (
        lax.all_to_all(query_buffer, "seq", split_axis=0, concat_axis=0, tiled=True),
        lax.all_to_all(value_buffer, "seq", split_axis=0, concat_axis=0, tiled=True),
    )
    mixed_list = []
    log_list = []
    for turn_index in range(ROUNDS):
        mixed_rows, log_total = forward_rows(
            sorted_rows(got_queries, turn_index),
            sorted_rows(got_values, turn_index),
            live_list[turn_index],
        )
        mixed_list.append(unsorted(mixed_rows, turn_index))
        log_list.append(unsorted(log_total, turn_index))
    back_mixed, back_logs = (
        lax.all_to_all(
            jnp.stack(mixed_list, axis=1), "seq", split_axis=0, concat_axis=0, tiled=True
        ),
        lax.all_to_all(jnp.stack(log_list, axis=1), "seq", split_axis=0, concat_axis=0, tiled=True),
    )
    turn_mixed = jnp.stack([home_rows(back_mixed, turn_index) for turn_index in range(ROUNDS)])
    turn_logs = jnp.stack([home_rows(back_logs, turn_index) for turn_index in range(ROUNDS)])
    largest = jnp.max(turn_logs, axis=0)
    log_all = largest + jnp.log(jnp.sum(jnp.exp(turn_logs - largest), axis=0))
    mix_weights = jnp.exp(turn_logs - log_all)
    combined = jnp.sum(mix_weights[..., None] * turn_mixed, axis=0)
    output = combined.reshape(tokens_here, width_here).astype(jnp.bfloat16)
    out_grads = out_cotangent.reshape(tokens_here, heads_here, HEAD_DIM)
    out_inner = jnp.sum(out_grads.astype(jnp.float32) * combined, axis=-1)
    weight_buffer = jnp.stack(
        [
            spread_rows(mix_weights[turn_index], source_list[turn_index]).reshape(
                seq_count, capacity, heads_here
            )
            for turn_index in range(ROUNDS)
        ],
        axis=1,
    )
    inner_buffer = pack_rows(out_inner)
    got_mixes, got_inners = (
        lax.all_to_all(weight_buffer, "seq", split_axis=0, concat_axis=0, tiled=True),
        lax.all_to_all(inner_buffer, "seq", split_axis=0, concat_axis=0, tiled=True),
    )
    grad_buffer = pack_rows(out_grads)
    back_queries, back_values, got_grads = (
        lax.all_to_all(query_buffer, "seq", split_axis=0, concat_axis=0, tiled=True),
        lax.all_to_all(value_buffer, "seq", split_axis=0, concat_axis=0, tiled=True),
        lax.all_to_all(grad_buffer, "seq", split_axis=0, concat_axis=0, tiled=True),
    )
    query_list = []
    value_list = []
    for turn_index in range(ROUNDS):
        query_turn, value_turn = backward_rows(
            sorted_rows(back_queries, turn_index),
            sorted_rows(back_values, turn_index),
            live_list[turn_index],
            sorted_rows(got_grads, turn_index),
            sorted_rows(got_mixes, turn_index),
            sorted_rows(got_inners, turn_index),
        )
        query_list.append(unsorted(query_turn, turn_index))
        value_list.append(unsorted(value_turn, turn_index))
    back_query, back_value = (
        lax.all_to_all(
            jnp.stack(query_list, axis=1), "seq", split_axis=0, concat_axis=0, tiled=True
        ),
        lax.all_to_all(
            jnp.stack(value_list, axis=1), "seq", split_axis=0, concat_axis=0, tiled=True
        ),
    )
    query_sum = home_rows(back_query, 0).astype(jnp.float32)
    value_sum = home_rows(back_value, 0).astype(jnp.float32)
    turn_index = 1
    query_sum = query_sum + home_rows(back_query, turn_index).astype(jnp.float32)
    value_sum = value_sum + home_rows(back_value, turn_index).astype(jnp.float32)
    query_grad = query_sum.reshape(tokens_here, width_here).astype(jnp.bfloat16)
    value_grad = value_sum.reshape(tokens_here, width_here).astype(jnp.bfloat16)
    contract_cols = (((1,), (1,)), ((), ()))
    terms = lax.dot_general(
        query_grad, full_weights[0], contract_cols, preferred_element_type=jnp.float32
    ) + lax.dot_general(
        value_grad, full_weights[1], contract_cols, preferred_element_type=jnp.float32
    )
    input_grad = lax.psum_scatter(
        terms.astype(jnp.bfloat16), "head", scatter_dimension=1, tiled=True
    )
    contract_rows = (((0,), (0,)), ((), ()))
    query_part = lax.dot_general(
        features, query_grad, contract_rows, preferred_element_type=jnp.float32
    )
    value_part = lax.dot_general(
        features, value_grad, contract_rows, preferred_element_type=jnp.float32
    )
    weight_grads = lax.psum_scatter(
        jnp.stack((query_part, value_part), axis=1).astype(jnp.bfloat16),
        "seq",
        scatter_dimension=0,
        tiled=True,
    ).astype(jnp.float32)
    return (output, input_grad, weight_grads[:, 0], weight_grads[:, 1])


def solution(mesh):
    return jax.shard_map(
        per_device,
        mesh=mesh,
        in_specs=(
            P("seq", "head"),
            P("seq", "head"),
            P("seq", "head"),
            P(None, "seq", None),
            P(None, "seq"),
            P("seq", "head"),
        ),
        out_specs=(P("seq", "head"), P("seq", "head"), P("seq", "head"), P("seq", "head")),
        check_vma=False,
    )
```

profile of v0, /device:TPU:8, one launch (start us, length us, event | category | flops | bytes accessed | tf_op | source)
XLA Modules:
  0.0 559.9 jit_solution(9881908167255207444)
XLA Ops:
  13.9 2.4 scatter_custom_fusion
  16.4 2.4 scatter_custom_fusion.1
  19.6 7.4 %all-to-all-start = ((s32[16,2,48]{2,1,0:T(2,128)}), s32[16,2,48]{2,1,0:T(2,128)S(1)}, u32[]{:S(2)}, u32[]{:S(2)}) async-start(s32[16,2,48]{2,1,0:T(2,128)} %pad_add_fusion), calls=%async_computation | async-start | bytes 32768 | tf_op jit(solution)/shard_map/all_to_all | solution.py:161
  27.0 2.4 scatter_custom_fusion.3
  29.5 2.9 scatter_custom_fusion.2
  32.7 2.9 gather_fusion.22
  35.6 2.9 gather_fusion.21
  42.5 4.4 sort.64
  46.9 3.2 gather_fusion.5
  50.1 4.4 sort.65
  54.4 4.4 sort.62
  58.8 3.2 gather_fusion
  62.1 64.8 %all-gather.3.cloned.1.call-done = bf16[2,4096,256]{1,2,0:T(8,128)(2,1)} async-done(((bf16[2,256,256]{1,2,0:T(8,128)(2,1)}), bf16[2,4096,256]{1,2,0:T(8,128)(2,1)}) %all-gather.3.cloned.1.call-update) | async-done | bytes 4194320 | tf_op jit(solution)/shard_map/all_gather | solution.py:131
  126.9 5.8 %fusion.12 = bf16[512,2,256]{0,2,1:T(8,128)(2,1)S(1)} fusion(bf16[2,4096,256]{1,2,0:T(8,128)(2,1)} %all-gather.3.cloned.1.call-done, bf16[512,4096]{1,0:T(8,128)(2,1)} %all-gather.5.cloned.1.call-done), kind=kOutput, calls=%fused_computation.75 | convolution fusion | flops 2147745792 | bytes 8912896 | tf_op jit(solution)/shard_map/td,kdc->tkc/dot_general | solution.py:132
  133.2 2.9 gather_fusion.2
  136.1 2.9 gather_fusion.1
  140.2 5.8 %all-to-all-start.1 = ((bf16[16,2,48,2,128]{4,2,3,1,0:T(8,128)(2,1)}), bf16[16,2,48,2,128]{4,2,3,1,0:T(8,128)(2,1)S(1)}, u32[]{:S(2)}, u32[]{:S(2)}) async-start(bf16[16,2,48,2,128]{4,2,3,1,0:T(8,128)(2,1)} %copy.474), calls=%async_computation.1 | async-start | bytes 1572864 | tf_op jit(solution)/shard_map/all_to_all | solution.py:203
  146.5 4.4 sort.63
  152.5 2.9 gather_fusion.11
  155.4 2.9 gather_fusion.10
  159.6 7.5 %all-to-all-start.3 = ((bf16[16,2,48,2,128]{4,2,3,1,0:T(8,128)(2,1)}), bf16[16,2,48,2,128]{4,2,3,1,0:T(8,128)(2,1)S(1)}, u32[]{:S(2)}, u32[]{:S(2)}) async-start(bf16[16,2,48,2,128]{4,2,3,1,0:T(8,128)(2,1)} %copy.507), calls=%async_computation.3 | async-start | bytes 1572864 | tf_op jit(solution)/shard_map/all_to_all | solution.py:204
  167.6 2.9 gather_fusion.3
  172.4 2.9 gather_fusion.6
  179.0 2.9 gather_fusion.12
  182.6 2.9 gather_fusion.14
  199.6 2.5 gather_fusion.4
  204.8 7.2 %all-to-all-start.2 = ((f32[16,1,192]{2,1,0:T(1,128)}), f32[16,1,192]{2,1,0:T(1,128)}, u32[]{:S(2)}, u32[]{:S(2)}) async-start(f32[16,1,192]{2,1,0:T(1,128)} %reshape.780), calls=%async_computation.2 | async-start | bytes 32768 | tf_op jit(solution)/shard_map/all_to_all | solution.py:220
  212.1 2.3 convolution_bitcast_fusion.6
  216.7 3.2 gather_fusion.15
  220.7 3.2 gather_fusion.13
  223.9 7.2 %all-to-all-start.6 = ((bf16[16,2,48,2,128]{4,3,2,1,0:T(2,128)(2,1)}), bf16[16,2,48,2,128]{4,3,2,1,0:T(2,128)(2,1)S(1)}, u32[]{:S(2)}, u32[]{:S(2)}) async-start(bf16[16,2,48,2,128]{4,3,2,1,0:T(2,128)(2,1)} %pad_maximum_fusion.4), calls=%async_computation.6 | async-start | bytes 1572864 | tf_op jit(solution)/shard_map/all_to_all | solution.py:249
  245.4 7.2 %all-to-all-start.5 = ((f32[16,1,192]{2,1,0:T(1,128)}), f32[16,1,192]{2,1,0:T(1,128)S(1)}, u32[]{:S(2)}, u32[]{:S(2)}) async-start(f32[16,1,192]{2,1,0:T(1,128)} %reshape.784), calls=%async_computation.5 | async-start | bytes 32768 | tf_op jit(solution)/shard_map/all_to_all | solution.py:242
  252.6 3.3 pad_maximum_fusion.1
  255.9 3.0 all-to-all-done.5
  259.5 5.0 all-to-all-start.4
  264.4 2.5 fusion.79
  267.0 2.8 gather_fusion.23
  270.5 2.8 gather_fusion.29
  280.6 2.5 convolution_bitcast_fusion
  285.7 2.7 gather_fusion.20
  289.5 2.6 convolution_bitcast_fusion.1
  297.1 3.5 gather_fusion.35
  305.2 3.6 gather_fusion.34
  310.2 2.7 gather_fusion.16
  312.9 2.7 gather_fusion.17
  315.5 3.1 fusion.15
  324.5 7.3 %all-to-all-start.7 = ((f32[16,1,192]{2,1,0:T(1,128)}), f32[16,1,192]{2,1,0:T(1,128)S(1)}, u32[]{:S(2)}, u32[]{:S(2)}) async-start(f32[16,1,192]{2,1,0:T(1,128)} %reshape.782), calls=%async_computation.7 | async-start | bytes 32768 | tf_op jit(solution)/shard_map/all_to_all | solution.py:243
  333.7 4.3 all-to-all-done.7
  338.0 5.8 %all-to-all-start.9 = ((bf16[16,2,48,2,128]{4,3,2,1,0:T(2,128)(2,1)}), bf16[16,2,48,2,128]{4,3,2,1,0:T(2,128)(2,1)}, u32[]{:S(2)}, u32[]{:S(2)}) async-start(bf16[16,2,48,2,128]{4,3,2,1,0:T(2,128)(2,1)} %pad_maximum_fusion.6), calls=%async_computation.9 | async-start | bytes 1572864 | tf_op jit(solution)/shard_map/all_to_all | solution.py:268
  345.5 2.3 gather_fusion.30
  354.0 2.3 gather_fusion.26
  357.5 2.8 select_convert_fusion.1
  365.8 2.9 gather_fusion.27
  369.7 2.9 gather_fusion.31
  374.6 7.3 %all-to-all-start.8 = ((bf16[16,2,48,2,128]{4,3,2,1,0:T(2,128)(2,1)}), bf16[16,2,48,2,128]{4,3,2,1,0:T(2,128)(2,1)S(1)}, u32[]{:S(2)}, u32[]{:S(2)}) async-start(bf16[16,2,48,2,128]{4,3,2,1,0:T(2,128)(2,1)} %pad_maximum_fusion.5), calls=%async_computation.8 | async-start | bytes 1572864 | tf_op jit(solution)/shard_map/all_to_all | solution.py:265
  383.6 2.3 gather_fusion.36
  388.3 3.4 fusion.1
  393.3 2.3 gather_fusion.32
  398.0 3.4 fusion
  401.5 2.3 pad_maximum_fusion
  403.9 3.0 fusion.4
  406.9 3.3 add_convert_fusion
  411.9 75.5 %reduce-scatter.5.cloned.1.call-done = bf16[256,2,256]{0,2,1:T(8,128)(2,1)} async-done(((bf16[4096,2,256]{0,2,1:T(8,128)(2,1)}), bf16[256,2,256]{0,2,1:T(8,128)(2,1)}) %reduce-scatter.5.cloned.1.call-update) | async-done | bytes 262160 | tf_op jit(solution)/shard_map/reduce_scatter | solution.py:295
  490.1 63.1 %reduce-scatter.3.cloned.1.call-done = bf16[512,256]{1,0:T(8,128)(2,1)} async-done(((bf16[512,4096]{1,0:T(8,128)(2,1)}), bf16[512,256]{1,0:T(8,128)(2,1)}) %reduce-scatter.3.cloned.1.call-update) | async-done | bytes 262160 | tf_op jit(solution)/shard_map/reduce_scatter | solution.py:285
  (392 shorter events, 117.7 us)
Async XLA Ops:
  7.2 3.6 copy-start.70
  7.2 6.7 %copy-start.73 = (s32[2,512]{1,0:T(2,128)S(1)}, s32[2,512]{1,0:T(2,128)}, u32[]{:S(2)}) copy-start(s32[2,512]{1,0:T(2,128)} %param.10) | copy-start | bytes 12292
  7.2 25.2 %copy-start.33 = (bf16[512,256]{1,0:T(8,128)(2,1)S(1)}, bf16[512,256]{1,0:T(8,128)(2,1)}, u32[]{:S(2)}) copy-start(bf16[512,256]{1,0:T(8,128)(2,1)} %param.11) | copy-start | bytes 786436
  7.2 54.9 %all-gather.5.cloned.1.call-start = ((), (), s32[]{:S(2)}) async-start(), calls=%async_computation.13 | async-start | bytes 4456448 | tf_op jit(solution)/shard_map/all_gather | solution.py:129
  7.9 119.0 %all-gather.3.cloned.1.call-start = ((), (), s32[]{:S(2)}) async-start(), calls=%async_computation.12 | async-start | bytes 4456448 | tf_op jit(solution)/shard_map/all_gather | solution.py:131
  19.6 22.7 %all-to-all-start = ((s32[16,2,48]{2,1,0:T(2,128)}), s32[16,2,48]{2,1,0:T(2,128)S(1)}, u32[]{:S(2)}, u32[]{:S(2)}) async-start(s32[16,2,48]{2,1,0:T(2,128)} %pad_add_fusion), calls=%async_computation | async-start | bytes 32768 | tf_op jit(solution)/shard_map/all_to_all | solution.py:161
  32.5 9.2 %copy-start.8 = (bf16[512,2,128]{2,1,0:T(2,128)(2,1)}, bf16[512,2,128]{2,1,0:T(2,128)(2,1)S(1)}, u32[]{:S(2)}) copy-start(bf16[512,2,128]{2,1,0:T(2,128)(2,1)S(1)} %reshape.381) | copy-start | bytes 786436
  35.6 119.8 %copy-start.34 = (s32[1024]{0:T(1024)}, s32[1024]{0:T(1024)S(1)}, u32[]{:S(2)}) copy-start(s32[1024]{0:T(1024)S(1)} %pad_clamp_fusion.6) | copy-start | bytes 12292
  140.2 19.4 %all-to-all-start.1 = ((bf16[16,2,48,2,128]{4,2,3,1,0:T(8,128)(2,1)}), bf16[16,2,48,2,128]{4,2,3,1,0:T(8,128)(2,1)S(1)}, u32[]{:S(2)}, u32[]{:S(2)}) async-start(bf16[16,2,48,2,128]{4,2,3,1,0:T(8,128)(2,1)} %copy.474), calls=%async_computation.1 | async-start | bytes 1572864 | tf_op jit(solution)/shard_map/all_to_all | solution.py:203
  151.5 65.2 %copy-start.36 = (s32[1024]{0:T(1024)}, s32[1024]{0:T(1024)S(1)}, u32[]{:S(2)}) copy-start(s32[1024]{0:T(1024)S(1)} %pad_clamp_fusion.2) | copy-start | bytes 12292
  159.6 18.9 %all-to-all-start.3 = ((bf16[16,2,48,2,128]{4,2,3,1,0:T(8,128)(2,1)}), bf16[16,2,48,2,128]{4,2,3,1,0:T(8,128)(2,1)S(1)}, u32[]{:S(2)}, u32[]{:S(2)}) async-start(bf16[16,2,48,2,128]{4,2,3,1,0:T(8,128)(2,1)} %copy.507), calls=%async_computation.3 | async-start | bytes 1572864 | tf_op jit(solution)/shard_map/all_to_all | solution.py:204
  175.6 1.8 copy-start.50
  177.4 13.2 %copy-start.29 = (bf16[640,2,128]{2,0,1:T(8,128)(2,1)}, bf16[640,2,128]{2,0,1:T(8,128)(2,1)S(1)}, u32[]{:S(2)}) copy-start(bf16[640,2,128]{2,0,1:T(8,128)(2,1)S(1)} %slice.414) | copy-start | bytes 983044
  178.1 12.5 %copy-start.40 = (bf16[1,128,2,128]{3,1,2,0:T(8,128)(2,1)}, bf16[1,128,2,128]{3,1,2,0:T(8,128)(2,1)S(1)}, u32[]{:S(2)}) copy-start(bf16[1,128,2,128]{3,1,2,0:T(8,128)(2,1)S(1)} %slice_bitcast_fusion.8) | copy-start | bytes 196612
  185.8 4.5 copy-start.69
  187.2 3.4 copy-start.60
  187.2 3.4 copy-start.74
  191.3 2.9 copy-start.66
  192.5 1.8 copy-start.67
  192.7 2.4 copy-start.68
  197.0 17.4 %copy-start.10 = (f32[6,2,128,256]{3,2,1,0:T(8,128)}, f32[6,2,128,256]{3,2,1,0:T(8,128)S(1)}, u32[]{:S(2)}) copy-start(f32[6,2,128,256]{3,2,1,0:T(8,128)S(1)} %get-tuple-element.85) | copy-start | bytes 4718596
  204.8 19.2 %all-to-all-start.2 = ((f32[16,1,192]{2,1,0:T(1,128)}), f32[16,1,192]{2,1,0:T(1,128)}, u32[]{:S(2)}, u32[]{:S(2)}) async-start(f32[16,1,192]{2,1,0:T(1,128)} %reshape.780), calls=%async_computation.2 | async-start | bytes 32768 | tf_op jit(solution)/shard_map/all_to_all | solution.py:220
  212.0 2.4 copy-start.26
  212.0 2.4 copy-start.32
  212.0 2.4 copy-start.43
  212.0 2.4 copy-start.62
  212.1 2.4 copy-start.65
  216.1 3.9 copy-start.19
  220.7 12.8 %copy-start.54 = (s32[1024]{0:T(1024)S(1)}, s32[1024]{0:T(1024)}, u32[]{:S(2)}) copy-start(s32[1024]{0:T(1024)} %pad_clamp_fusion) | copy-start | bytes 12292
  223.9 21.5 %all-to-all-start.6 = ((bf16[16,2,48,2,128]{4,3,2,1,0:T(2,128)(2,1)}), bf16[16,2,48,2,128]{4,3,2,1,0:T(2,128)(2,1)S(1)}, u32[]{:S(2)}, u32[]{:S(2)}) async-start(bf16[16,2,48,2,128]{4,3,2,1,0:T(2,128)(2,1)} %pad_maximum_fusion.4), calls=%async_computation.6 | async-start | bytes 1572864 | tf_op jit(solution)/shard_map/all_to_all | solution.py:249
  236.7 2.7 copy-start
  241.2 3.5 copy-start.45
  241.2 11.5 %copy-start.4 = (f32[768,2,128]{2,1,0:T(2,128)S(1)}, f32[768,2,128]{2,1,0:T(2,128)}, u32[]{:S(2)}) copy-start(f32[768,2,128]{2,1,0:T(2,128)} %gather_fusion.15) | copy-start | bytes 2359300
  245.4 10.5 %copy-start.3 = (bf16[16,2,48,2,128]{4,3,2,1,0:T(2,128)(2,1)}, bf16[16,2,48,2,128]{4,3,2,1,0:T(2,128)(2,1)S(1)}, u32[]{:S(2)}) copy-start(bf16[16,2,48,2,128]{4,3,2,1,0:T(2,128)(2,1)S(1)} %all-to-all-done.6) | copy-start | bytes 2359300
  245.4 13.5 %all-to-all-start.5 = ((f32[16,1,192]{2,1,0:T(1,128)}), f32[16,1,192]{2,1,0:T(1,128)S(1)}, u32[]{:S(2)}, u32[]{:S(2)}) async-start(f32[16,1,192]{2,1,0:T(1,128)} %reshape.784), calls=%async_computation.5 | async-start | bytes 32768 | tf_op jit(solution)/shard_map/all_to_all | solution.py:242
  259.5 49.4 %all-to-all-start.4 = ((f32[16,2,48,2,128]{4,3,2,1,0:T(2,128)}), f32[16,2,48,2,128]{4,3,2,1,0:T(2,128)S(1)}, u32[]{:S(2)}, u32[]{:S(2)}) async-start(f32[16,2,48,2,128]{4,3,2,1,0:T(2,128)} %pad_maximum_fusion.1), calls=%async_computation.4 | async-start | bytes 3145728 | tf_op jit(solution)/shard_map/all_to_all | solution.py:217
  280.6 2.5 copy-start.72
  283.2 1.6 copy-start.13
  289.5 2.6 copy-start.71
  289.5 4.2 copy-start.14
  292.2 1.7 copy-start.23
  293.8 3.3 copy-start.37
  308.8 4.0 copy-start.55
  310.2 5.4 copy-start.1
  312.9 5.8 %copy-start.9 = (bf16[512,2,128]{2,1,0:T(2,128)(2,1)S(1)}, bf16[512,2,128]{2,1,0:T(2,128)(2,1)}, u32[]{:S(2)}) copy-start(bf16[512,2,128]{2,1,0:T(2,128)(2,1)} %copy-done.8) | copy-start | bytes 786436
  321.8 10.0 %copy-start.16 = (bf16[768,2,128]{2,1,0:T(2,128)(2,1)S(1)}, bf16[768,2,128]{2,1,0:T(2,128)(2,1)}, u32[]{:S(2)}) copy-start(bf16[768,2,128]{2,1,0:T(2,128)(2,1)} %gather_fusion.35) | copy-start | bytes 1179652
  321.8 10.0 %copy-start.17 = (bf16[768,2,128]{2,1,0:T(2,128)(2,1)S(1)}, bf16[768,2,128]{2,1,0:T(2,128)(2,1)}, u32[]{:S(2)}) copy-start(bf16[768,2,128]{2,1,0:T(2,128)(2,1)} %gather_fusion.34) | copy-start | bytes 1179652
  324.5 13.5 %all-to-all-start.7 = ((f32[16,1,192]{2,1,0:T(1,128)}), f32[16,1,192]{2,1,0:T(1,128)S(1)}, u32[]{:S(2)}, u32[]{:S(2)}) async-start(f32[16,1,192]{2,1,0:T(1,128)} %reshape.782), calls=%async_computation.7 | async-start | bytes 32768 | tf_op jit(solution)/shard_map/all_to_all | solution.py:243
  338.0 36.6 %all-to-all-start.9 = ((bf16[16,2,48,2,128]{4,3,2,1,0:T(2,128)(2,1)}), bf16[16,2,48,2,128]{4,3,2,1,0:T(2,128)(2,1)}, u32[]{:S(2)}, u32[]{:S(2)}) async-start(bf16[16,2,48,2,128]{4,3,2,1,0:T(2,128)(2,1)} %pad_maximum_fusion.6), calls=%async_computation.9 | async-start | bytes 1572864 | tf_op jit(solution)/shard_map/all_to_all | solution.py:268
  345.5 3.4 copy-start.12
  351.1 2.0 copy-start.20
  354.0 3.4 copy-start.63
  357.4 2.8 copy-start.28
  357.4 2.8 copy-start.31
  357.5 2.8 copy-start.42
  365.1 3.6 copy-start.5
  365.2 3.6 copy-start.51
  365.2 3.6 copy-start.47
  374.6 9.0 %copy-start.59 = (s32[1024]{0:T(1024)S(1)}, s32[1024]{0:T(1024)}, u32[]{:S(2)}) copy-start(s32[1024]{0:T(1024)} %pad_clamp_fusion.1) | copy-start | bytes 12292
  374.6 11.4 %copy-start.56 = (s32[1024]{0:T(1024)S(1)}, s32[1024]{0:T(1024)}, u32[]{:S(2)}) copy-start(s32[1024]{0:T(1024)} %pad_clamp_fusion) | copy-start | bytes 12292
  374.6 17.4 %all-to-all-start.8 = ((bf16[16,2,48,2,128]{4,3,2,1,0:T(2,128)(2,1)}), bf16[16,2,48,2,128]{4,3,2,1,0:T(2,128)(2,1)S(1)}, u32[]{:S(2)}, u32[]{:S(2)}) async-start(bf16[16,2,48,2,128]{4,3,2,1,0:T(2,128)(2,1)} %pad_maximum_fusion.5), calls=%async_computation.8 | async-start | bytes 1572864 | tf_op jit(solution)/shard_map/all_to_all | solution.py:265
  381.9 105.5 %reduce-scatter.5.cloned.1.call-start = ((), (), s32[]{:S(2)}) async-start(), calls=%async_computation.15 | async-start | bytes 4456448 | tf_op jit(solution)/shard_map/reduce_scatter | solution.py:295
  403.8 149.3 %reduce-scatter.3.cloned.1.call-start = ((), (), s32[]{:S(2)}) async-start(), calls=%async_computation.14 | async-start | bytes 4456448 | tf_op jit(solution)/shard_map/reduce_scatter | solution.py:285
  403.9 3.0 copy-start.2
  (25 other events, 26.9 us)
Sparse Core Ops, SparseCore 0:
  9.8 51.8 all-gather.4
  64.7 62.1 all-gather.2
  404.0 83.3 reduce-scatter.4
  490.5 62.5 reduce-scatter.2
where the time goes:
time: 567 us; the launch traced here: 560 us
  waiting for transfers between devices  212 us (37%)
  local copies, waits for them, and re-layouts  171 us (30%)
  starting transfers between devices  67.8 us (12%)
  other arithmetic  56.9 us (10%)
  matrix products  36.6 us (6%)
  between operations  16 us (3%)
    reduce_scatter x1, waiting for transfers between devices, per_device(): lax.psum_scatter(jnp.stack((query_part, value_part), axis=1).astype(jnp.b...  75.5 us
    all_gather x1, waiting for transfers between devices, per_device(): full_weights = lax.all_gather(stacked, 'seq', axis=1, tiled=True)  64.8 us
    reduce_scatter x1, waiting for transfers between devices, per_device(): lax.psum_scatter(terms.astype(jnp.bfloat16), 'head', scatter_dimension=1,...  63.1 us
    gather x14, local copies, waits for them, and re-layouts, sorted_rows(): buffer[:, turn_index].reshape((slot_count,) + buffer.shape[3:])  28.3 us
    gather x14, local copies, waits for them, and re-layouts, spread_rows(): return padded[source_rows]  24.8 us
    gather x8, local copies, waits for them, and re-layouts, unsorted(): token_rows[inverses[turn_index]]  23.4 us
    gather x10, local copies, waits for them, and re-layouts, home_rows(): buffer[:, turn_index].reshape((slot_count,) + buffer.shape[3:])  16.5 us
    unnamed x167, local copies, waits for them, and re-layouts  13.6 us
  transfers between devices with their start and end apart: 14, of which 7 were waited for; matrix products, arithmetic and copies ran while one was open for 35% of the time, Pallas kernels for 0%

commit v1 on v0

--- a/solution.py
+++ b/solution.py
@@ -128,7 +128,9 @@
     slot_count = seq_count * capacity
     features = lax.all_gather(layer_input, "head", axis=1, tiled=True)
     stacked = jnp.stack((qk_weight, value_weight))
-    full_weights = lax.all_gather(stacked, "seq", axis=1, tiled=True)
+    full_weights = jnp.concatenate(
+        lax.all_to_all(jnp.stack([stacked] * lax.axis_size("seq")), "seq", 0, 0), axis=1
+    )
     projected = jnp.einsum(
         "td,kdc->tkc", features, full_weights, preferred_element_type=jnp.float32
     )

time: 567 us -> 549 us (0.968)
  waiting for transfers between devices: 212 us -> 165 us
  local copies, waits for them, and re-layouts: 171 us -> 185 us
  starting transfers between devices: 67.8 us -> 81.6 us
    all_gather x1 -> x0, waiting for transfers between devices: 64.8 us -> none  [per_device(): full_weights = lax.all_gather(stacked, 'seq', axis=1, tiled=True)]
    all_to_all x0 -> x1, waiting for transfers between devices: none -> 23.6 us  [per_device(): lax.all_to_all(jnp.stack([stacked] * lax.axis_size('seq')), 'seq', 0, 0)]
    all_to_all x0 -> x1, starting transfers between devices: none -> 7.84 us  [per_device(): lax.all_to_all(jnp.stack([stacked] * lax.axis_size('seq')), 'seq', 0, 0)]
    all_to_all x0 -> x1, local copies, waits for them, and re-layouts: none -> 6.28 us  [per_device(): lax.all_to_all(jnp.stack([stacked] * lax.axis_size('seq')), 'seq', 0, 0)]
    all_to_all x1, starting transfers between devices: 5.76 us -> 11.4 us  [per_device(): lax.all_to_all(query_buffer, 'seq', split_axis=0, concat_axis=0, tiled=True)]
    unnamed x167 -> x153, local copies, waits for them, and re-layouts: 13.6 us -> 11.6 us
  transfers between devices with their start and end apart: 14 -> 14, of which waited for: 7 -> 6; matrix products, arithmetic and copies ran while one was open for 35% -> 39% of each run, Pallas kernels for 0% -> 0%
where the time goes in v1:
time: 549 us; the launch traced here: 541 us
  local copies, waits for them, and re-layouts  185 us (34%)
  waiting for transfers between devices  165 us (30%)
  starting transfers between devices  81.6 us (15%)
  other arithmetic  58.9 us (11%)
  matrix products  34.9 us (6%)
  between operations  15.8 us (3%)
    reduce_scatter x1, waiting for transfers between devices, per_device(): lax.psum_scatter(jnp.stack((query_part, value_part), axis=1).astype(jnp.b...  70 us
    reduce_scatter x1, waiting for transfers between devices, per_device(): lax.psum_scatter(terms.astype(jnp.bfloat16), 'head', scatter_dimension=1,...  63.1 us
    gather x14, local copies, waits for them, and re-layouts, sorted_rows(): buffer[:, turn_index].reshape((slot_count,) + buffer.shape[3:])  28.3 us
    gather x14, local copies, waits for them, and re-layouts, spread_rows(): return padded[source_rows]  24.1 us
    all_to_all x1, waiting for transfers between devices, per_device(): lax.all_to_all(jnp.stack([stacked] * lax.axis_size('seq')), 'seq', 0, 0)  23.6 us
    gather x8, local copies, waits for them, and re-layouts, unsorted(): token_rows[inverses[turn_index]]  23.4 us
    gather x10, local copies, waits for them, and re-layouts, home_rows(): buffer[:, turn_index].reshape((slot_count,) + buffer.shape[3:])  16.5 us
    unnamed x153, local copies, waits for them, and re-layouts  11.6 us
  transfers between devices with their start and end apart: 14, of which 6 were waited for; matrix products, arithmetic and copies ran while one was open for 39% of the time, Pallas kernels for 0%

profile of v1, /device:TPU:8, one launch (start us, length us, event | category | flops | bytes accessed | tf_op | source)
XLA Modules:
  0.0 541.4 jit_solution(11178350300973509998)
XLA Ops:
  13.2 2.4 scatter_custom_fusion
  15.7 2.4 scatter_custom_fusion.1
  18.9 7.4 %all-to-all-start = ((s32[16,2,48]{2,1,0:T(2,128)}), s32[16,2,48]{2,1,0:T(2,128)S(1)}, u32[]{:S(2)}, u32[]{:S(2)}) async-start(s32[16,2,48]{2,1,0:T(2,128)} %pad_add_fusion), calls=%async_computation | async-start | bytes 32768 | tf_op jit(solution)/shard_map/all_to_all | solution.py:163
  27.2 2.4 scatter_custom_fusion.3
  29.7 2.4 scatter_custom_fusion.2
  33.6 2.4 stack.92
  36.0 7.8 %all-to-all-start.1 = ((bf16[16,2,256,256]{2,3,1,0:T(8,128)(2,1)}), bf16[16,2,256,256]{2,3,1,0:T(8,128)(2,1)}, u32[]{:S(2)}, u32[]{:S(2)}) async-start(bf16[16,2,256,256]{2,3,1,0:T(8,128)(2,1)} %stack.92), calls=%async_computation.1 | async-start | bytes 8388608 | tf_op jit(solution)/shard_map/all_to_all | solution.py:132
  43.9 2.9 gather_fusion.22
  46.8 2.9 gather_fusion.21
  53.7 4.4 sort.64
  58.1 3.2 gather_fusion.5
  61.3 4.4 sort.65
  65.6 4.4 sort.62
  70.0 3.2 gather_fusion
  73.3 23.6 %all-to-all-done.1 = bf16[16,2,256,256]{2,3,1,0:T(8,128)(2,1)} async-done(((bf16[16,2,256,256]{2,3,1,0:T(8,128)(2,1)}), bf16[16,2,256,256]{2,3,1,0:T(8,128)(2,1)}, u32[]{:S(2)}, u32[]{:S(2)}) %all-to-all-start.1) | async-done | bytes 4194336 | tf_op jit(solution)/shard_map/all_to_all | solution.py:132
  96.9 4.7 copy.703
  101.7 5.8 %fusion.11 = bf16[512,2,256]{0,2,1:T(8,128)(2,1)S(1)} fusion(bf16[2,4096,256]{1,2,0:T(8,128)(2,1)} %bitcast.276, bf16[512,4096]{1,0:T(8,128)(2,1)} %all-gather.2.cloned.1.call-done), kind=kOutput, calls=%fused_computation.72 | convolution fusion | flops 2147745792 | bytes 8912896 | tf_op jit(solution)/shard_map/td,kdc->tkc/dot_general | solution.py:134
  107.9 2.9 gather_fusion.2
  110.8 2.9 gather_fusion.1
  114.9 11.4 %all-to-all-start.2 = ((bf16[16,2,48,2,128]{4,2,3,1,0:T(8,128)(2,1)}), bf16[16,2,48,2,128]{4,2,3,1,0:T(8,128)(2,1)S(1)}, u32[]{:S(2)}, u32[]{:S(2)}) async-start(bf16[16,2,48,2,128]{4,2,3,1,0:T(8,128)(2,1)} %copy.577), calls=%async_computation.2 | async-start | bytes 1572864 | tf_op jit(solution)/shard_map/all_to_all | solution.py:205
  126.9 4.4 sort.63
  132.9 2.9 gather_fusion.11
  135.8 2.9 gather_fusion.10
  139.9 7.5 %all-to-all-start.4 = ((bf16[16,2,48,2,128]{4,2,3,1,0:T(8,128)(2,1)}), bf16[16,2,48,2,128]{4,2,3,1,0:T(8,128)(2,1)S(1)}, u32[]{:S(2)}, u32[]{:S(2)}) async-start(bf16[16,2,48,2,128]{4,2,3,1,0:T(8,128)(2,1)} %copy.610), calls=%async_computation.4 | async-start | bytes 1572864 | tf_op jit(solution)/shard_map/all_to_all | solution.py:206
  147.9 2.9 gather_fusion.3
  152.7 2.9 gather_fusion.6
  158.9 2.9 gather_fusion.12
  162.6 2.9 gather_fusion.14
  179.6 2.4 gather_fusion.4
  184.7 7.6 %all-to-all-start.3 = ((f32[16,1,192]{2,1,0:T(1,128)}), f32[16,1,192]{2,1,0:T(1,128)}, u32[]{:S(2)}, u32[]{:S(2)}) async-start(f32[16,1,192]{2,1,0:T(1,128)} %reshape.794), calls=%async_computation.3 | async-start | bytes 32768 | tf_op jit(solution)/shard_map/all_to_all | solution.py:222
  197.0 3.2 gather_fusion.15
  200.9 3.2 gather_fusion.13
  204.2 7.2 %all-to-all-start.7 = ((bf16[16,2,48,2,128]{4,3,2,1,0:T(2,128)(2,1)}), bf16[16,2,48,2,128]{4,3,2,1,0:T(2,128)(2,1)S(1)}, u32[]{:S(2)}, u32[]{:S(2)}) async-start(bf16[16,2,48,2,128]{4,3,2,1,0:T(2,128)(2,1)} %pad_maximum_fusion.4), calls=%async_computation.7 | async-start | bytes 1572864 | tf_op jit(solution)/shard_map/all_to_all | solution.py:251
  225.2 7.2 %all-to-all-start.6 = ((f32[16,1,192]{2,1,0:T(1,128)}), f32[16,1,192]{2,1,0:T(1,128)S(1)}, u32[]{:S(2)}, u32[]{:S(2)}) async-start(f32[16,1,192]{2,1,0:T(1,128)} %reshape.798), calls=%async_computation.6 | async-start | bytes 32768 | tf_op jit(solution)/shard_map/all_to_all | solution.py:244
  232.4 3.5 pad_maximum_fusion.1
  235.9 2.7 all-to-all-done.6
  239.3 5.0 all-to-all-start.5
  244.2 2.6 fusion.79
  246.8 2.8 gather_fusion.23
  250.4 2.8 gather_fusion.29
  260.4 2.5 convolution_bitcast_fusion
  265.5 2.7 gather_fusion.20
  269.3 2.6 convolution_bitcast_fusion.1
  276.9 3.5 gather_fusion.35
  285.0 3.6 gather_fusion.34
  290.0 2.7 gather_fusion.16
  292.7 2.7 gather_fusion.17
  295.4 3.1 fusion.14
  304.3 7.3 %all-to-all-start.8 = ((f32[16,1,192]{2,1,0:T(1,128)}), f32[16,1,192]{2,1,0:T(1,128)S(1)}, u32[]{:S(2)}, u32[]{:S(2)}) async-start(f32[16,1,192]{2,1,0:T(1,128)} %reshape.796), calls=%async_computation.8 | async-start | bytes 32768 | tf_op jit(solution)/shard_map/all_to_all | solution.py:245
  313.6 4.3 all-to-all-done.8
  317.9 5.8 %all-to-all-start.10 = ((bf16[16,2,48,2,128]{4,3,2,1,0:T(2,128)(2,1)}), bf16[16,2,48,2,128]{4,3,2,1,0:T(2,128)(2,1)}, u32[]{:S(2)}, u32[]{:S(2)}) async-start(bf16[16,2,48,2,128]{4,3,2,1,0:T(2,128)(2,1)} %pad_maximum_fusion.6), calls=%async_computation.10 | async-start | bytes 1572864 | tf_op jit(solution)/shard_map/all_to_all | solution.py:270
  337.3 2.8 select_convert_fusion.1
  345.6 2.9 gather_fusion.27
  349.6 2.9 gather_fusion.31
  354.4 7.3 %all-to-all-start.9 = ((bf16[16,2,48,2,128]{4,3,2,1,0:T(2,128)(2,1)}), bf16[16,2,48,2,128]{4,3,2,1,0:T(2,128)(2,1)S(1)}, u32[]{:S(2)}, u32[]{:S(2)}) async-start(bf16[16,2,48,2,128]{4,3,2,1,0:T(2,128)(2,1)} %pad_maximum_fusion.5), calls=%async_computation.9 | async-start | bytes 1572864 | tf_op jit(solution)/shard_map/all_to_all | solution.py:267
  368.1 3.4 fusion.1
  373.2 2.3 gather_fusion.32
  377.8 3.4 fusion
  381.3 2.3 pad_maximum_fusion
  383.7 6.3 %copy.572 = bf16[16,2,256,256]{3,2,0,1:T(8,128)(2,1)} copy(bf16[16,2,256,256]{2,3,1,0:T(8,128)(2,1)} %all-to-all-done.1) | data formatting | bytes 8388608 | tf_op jit(solution)/shard_map/all_to_all | solution.py:132
  390.0 2.5 fusion.75
  393.9 3.3 add_convert_fusion
  398.9 70.0 %reduce-scatter.5.cloned.1.call-done = bf16[256,2,256]{0,2,1:T(8,128)(2,1)} async-done(((bf16[4096,2,256]{0,2,1:T(8,128)(2,1)}), bf16[256,2,256]{0,2,1:T(8,128)(2,1)}) %reduce-scatter.5.cloned.1.call-update) | async-done | bytes 262160 | tf_op jit(solution)/shard_map/reduce_scatter | solution.py:297
  471.6 63.1 %reduce-scatter.3.cloned.1.call-done = bf16[512,256]{1,0:T(8,128)(2,1)} async-done(((bf16[512,4096]{1,0:T(8,128)(2,1)}), bf16[512,256]{1,0:T(8,128)(2,1)}) %reduce-scatter.3.cloned.1.call-update) | async-done | bytes 262160 | tf_op jit(solution)/shard_map/reduce_scatter | solution.py:287
  (382 shorter events, 128.7 us)
Async XLA Ops:
  7.2 94.5 %all-gather.2.cloned.1.call-start = ((), (), s32[]{:S(2)}) async-start(), calls=%async_computation.13 | async-start | bytes 4456448 | tf_op jit(solution)/shard_map/all_gather | solution.py:129
  18.9 14.7 %all-to-all-start = ((s32[16,2,48]{2,1,0:T(2,128)}), s32[16,2,48]{2,1,0:T(2,128)S(1)}, u32[]{:S(2)}, u32[]{:S(2)}) async-start(s32[16,2,48]{2,1,0:T(2,128)} %pad_add_fusion), calls=%async_computation | async-start | bytes 32768 | tf_op jit(solution)/shard_map/all_to_all | solution.py:163
  33.2 2.8 copy-start.6
  36.0 60.9 %all-to-all-start.1 = ((bf16[16,2,256,256]{2,3,1,0:T(8,128)(2,1)}), bf16[16,2,256,256]{2,3,1,0:T(8,128)(2,1)}, u32[]{:S(2)}, u32[]{:S(2)}) async-start(bf16[16,2,256,256]{2,3,1,0:T(8,128)(2,1)} %stack.92), calls=%async_computation.1 | async-start | bytes 8388608 | tf_op jit(solution)/shard_map/all_to_all | solution.py:132
  46.8 89.0 %copy-start.31 = (s32[1024]{0:T(1024)}, s32[1024]{0:T(1024)S(1)}, u32[]{:S(2)}) copy-start(s32[1024]{0:T(1024)S(1)} %pad_clamp_fusion.6) | copy-start | bytes 12292
  114.9 25.0 %all-to-all-start.2 = ((bf16[16,2,48,2,128]{4,2,3,1,0:T(8,128)(2,1)}), bf16[16,2,48,2,128]{4,2,3,1,0:T(8,128)(2,1)S(1)}, u32[]{:S(2)}, u32[]{:S(2)}) async-start(bf16[16,2,48,2,128]{4,2,3,1,0:T(8,128)(2,1)} %copy.577), calls=%async_computation.2 | async-start | bytes 1572864 | tf_op jit(solution)/shard_map/all_to_all | solution.py:205
  131.9 65.1 %copy-start.33 = (s32[1024]{0:T(1024)}, s32[1024]{0:T(1024)S(1)}, u32[]{:S(2)}) copy-start(s32[1024]{0:T(1024)S(1)} %pad_clamp_fusion.2) | copy-start | bytes 12292
  139.9 18.5 %all-to-all-start.4 = ((bf16[16,2,48,2,128]{4,2,3,1,0:T(8,128)(2,1)}), bf16[16,2,48,2,128]{4,2,3,1,0:T(8,128)(2,1)S(1)}, u32[]{:S(2)}, u32[]{:S(2)}) async-start(bf16[16,2,48,2,128]{4,2,3,1,0:T(8,128)(2,1)} %copy.610), calls=%async_computation.4 | async-start | bytes 1572864 | tf_op jit(solution)/shard_map/all_to_all | solution.py:206
  155.9 1.8 copy-start.46
  157.7 12.8 %copy-start.27 = (bf16[640,2,128]{2,0,1:T(8,128)(2,1)}, bf16[640,2,128]{2,0,1:T(8,128)(2,1)S(1)}, u32[]{:S(2)}) copy-start(bf16[640,2,128]{2,0,1:T(8,128)(2,1)S(1)} %slice.416) | copy-start | bytes 983044
  158.4 12.1 %copy-start.37 = (bf16[1,128,2,128]{3,1,2,0:T(8,128)(2,1)}, bf16[1,128,2,128]{3,1,2,0:T(8,128)(2,1)S(1)}, u32[]{:S(2)}) copy-start(bf16[1,128,2,128]{3,1,2,0:T(8,128)(2,1)S(1)} %slice_bitcast_fusion.4) | copy-start | bytes 196612
  165.7 4.5 copy-start.65
  167.2 3.4 copy-start.56
  167.2 3.4 copy-start.68
  171.3 2.9 copy-start.62
  172.4 1.8 copy-start.63
  172.6 2.4 copy-start.64
  175.3 1.6 copy-start.25
  176.9 17.7 %copy-start.8 = (f32[6,2,128,256]{3,2,1,0:T(8,128)}, f32[6,2,128,256]{3,2,1,0:T(8,128)S(1)}, u32[]{:S(2)}) copy-start(f32[6,2,128,256]{3,2,1,0:T(8,128)S(1)} %get-tuple-element.91) | copy-start | bytes 4718596
  184.7 19.5 %all-to-all-start.3 = ((f32[16,1,192]{2,1,0:T(1,128)}), f32[16,1,192]{2,1,0:T(1,128)}, u32[]{:S(2)}, u32[]{:S(2)}) async-start(f32[16,1,192]{2,1,0:T(1,128)} %reshape.794), calls=%async_computation.3 | async-start | bytes 32768 | tf_op jit(solution)/shard_map/all_to_all | solution.py:222
  192.3 2.4 copy-start.24
  192.3 2.4 copy-start.30
  192.3 2.4 copy-start.40
  192.3 2.4 copy-start.58
  192.3 2.4 copy-start.61
  196.3 3.9 copy-start.17
  200.9 12.8 %copy-start.50 = (s32[1024]{0:T(1024)S(1)}, s32[1024]{0:T(1024)}, u32[]{:S(2)}) copy-start(s32[1024]{0:T(1024)} %pad_clamp_fusion) | copy-start | bytes 12292
  204.2 21.0 %all-to-all-start.7 = ((bf16[16,2,48,2,128]{4,3,2,1,0:T(2,128)(2,1)}), bf16[16,2,48,2,128]{4,3,2,1,0:T(2,128)(2,1)S(1)}, u32[]{:S(2)}, u32[]{:S(2)}) async-start(bf16[16,2,48,2,128]{4,3,2,1,0:T(2,128)(2,1)} %pad_maximum_fusion.4), calls=%async_computation.7 | async-start | bytes 1572864 | tf_op jit(solution)/shard_map/all_to_all | solution.py:251
  213.8 1.5 copy-start.53
  218.8 2.7 copy-start
  225.2 10.7 %copy-start.2 = (bf16[16,2,48,2,128]{4,3,2,1,0:T(2,128)(2,1)}, bf16[16,2,48,2,128]{4,3,2,1,0:T(2,128)(2,1)S(1)}, u32[]{:S(2)}) copy-start(bf16[16,2,48,2,128]{4,3,2,1,0:T(2,128)(2,1)S(1)} %all-to-all-done.7) | copy-start | bytes 2359300
  225.2 13.5 %all-to-all-start.6 = ((f32[16,1,192]{2,1,0:T(1,128)}), f32[16,1,192]{2,1,0:T(1,128)S(1)}, u32[]{:S(2)}, u32[]{:S(2)}) async-start(f32[16,1,192]{2,1,0:T(1,128)} %reshape.798), calls=%async_computation.6 | async-start | bytes 32768 | tf_op jit(solution)/shard_map/all_to_all | solution.py:244
  239.3 49.4 %all-to-all-start.5 = ((f32[16,2,48,2,128]{4,3,2,1,0:T(2,128)}), f32[16,2,48,2,128]{4,3,2,1,0:T(2,128)S(1)}, u32[]{:S(2)}, u32[]{:S(2)}) async-start(f32[16,2,48,2,128]{4,3,2,1,0:T(2,128)} %pad_maximum_fusion.1), calls=%async_computation.5 | async-start | bytes 3145728 | tf_op jit(solution)/shard_map/all_to_all | solution.py:219
  260.4 2.5 copy-start.67
  263.0 1.6 copy-start.11
  269.3 2.6 copy-start.66
  269.3 4.2 copy-start.12
  272.0 1.6 copy-start.13
  272.0 1.6 copy-start.5
  272.0 1.7 copy-start.21
  273.7 3.3 copy-start.34
  288.7 1.3 copy-start.54
  288.7 4.0 copy-start.51
  290.0 5.4 copy-start.1
  292.7 5.8 %copy-start.7 = (bf16[512,2,128]{2,1,0:T(2,128)(2,1)S(1)}, bf16[512,2,128]{2,1,0:T(2,128)(2,1)}, u32[]{:S(2)}) copy-start(bf16[512,2,128]{2,1,0:T(2,128)(2,1)} %copy-done.6) | copy-start | bytes 786436
  300.0 1.6 copy-start.32
  301.6 10.0 %copy-start.14 = (bf16[768,2,128]{2,1,0:T(2,128)(2,1)S(1)}, bf16[768,2,128]{2,1,0:T(2,128)(2,1)}, u32[]{:S(2)}) copy-start(bf16[768,2,128]{2,1,0:T(2,128)(2,1)} %gather_fusion.35) | copy-start | bytes 1179652
  301.6 10.0 %copy-start.15 = (bf16[768,2,128]{2,1,0:T(2,128)(2,1)S(1)}, bf16[768,2,128]{2,1,0:T(2,128)(2,1)}, u32[]{:S(2)}) copy-start(bf16[768,2,128]{2,1,0:T(2,128)(2,1)} %gather_fusion.34) | copy-start | bytes 1179652
  304.3 13.5 %all-to-all-start.8 = ((f32[16,1,192]{2,1,0:T(1,128)}), f32[16,1,192]{2,1,0:T(1,128)S(1)}, u32[]{:S(2)}, u32[]{:S(2)}) async-start(f32[16,1,192]{2,1,0:T(1,128)} %reshape.796), calls=%async_computation.8 | async-start | bytes 32768 | tf_op jit(solution)/shard_map/all_to_all | solution.py:245
  317.9 36.5 %all-to-all-start.10 = ((bf16[16,2,48,2,128]{4,3,2,1,0:T(2,128)(2,1)}), bf16[16,2,48,2,128]{4,3,2,1,0:T(2,128)(2,1)}, u32[]{:S(2)}, u32[]{:S(2)}) async-start(bf16[16,2,48,2,128]{4,3,2,1,0:T(2,128)(2,1)} %pad_maximum_fusion.6), calls=%async_computation.10 | async-start | bytes 1572864 | tf_op jit(solution)/shard_map/all_to_all | solution.py:270
  325.3 3.4 copy-start.10
  330.9 2.0 copy-start.18
  333.8 3.4 copy-start.59
  337.3 2.8 copy-start.26
  337.3 2.8 copy-start.29
  337.3 2.8 copy-start.39
  345.0 3.6 copy-start.3
  345.0 3.6 copy-start.47
  345.1 3.6 copy-start.43
  354.4 9.0 %copy-start.55 = (s32[1024]{0:T(1024)S(1)}, s32[1024]{0:T(1024)}, u32[]{:S(2)}) copy-start(s32[1024]{0:T(1024)} %pad_clamp_fusion.1) | copy-start | bytes 12292
  354.4 11.4 %copy-start.52 = (s32[1024]{0:T(1024)S(1)}, s32[1024]{0:T(1024)}, u32[]{:S(2)}) copy-start(s32[1024]{0:T(1024)} %pad_clamp_fusion) | copy-start | bytes 12292
  354.4 17.4 %all-to-all-start.9 = ((bf16[16,2,48,2,128]{4,3,2,1,0:T(2,128)(2,1)}), bf16[16,2,48,2,128]{4,3,2,1,0:T(2,128)(2,1)S(1)}, u32[]{:S(2)}, u32[]{:S(2)}) async-start(bf16[16,2,48,2,128]{4,3,2,1,0:T(2,128)(2,1)} %pad_maximum_fusion.5), calls=%async_computation.9 | async-start | bytes 1572864 | tf_op jit(solution)/shard_map/all_to_all | solution.py:267
  361.7 107.2 %reduce-scatter.5.cloned.1.call-start = ((), (), s32[]{:S(2)}) async-start(), calls=%async_computation.15 | async-start | bytes 4456448 | tf_op jit(solution)/shard_map/reduce_scatter | solution.py:297
  383.7 151.0 %reduce-scatter.3.cloned.1.call-start = ((), (), s32[]{:S(2)}) async-start(), calls=%async_computation.14 | async-start | bytes 4456448 | tf_op jit(solution)/shard_map/reduce_scatter | solution.py:287
  (19 other events, 17.7 us)
Sparse Core Ops, SparseCore 0:
  9.8 52.7 all-gather.1
  383.8 85.0 reduce-scatter.4
  472.2 62.4 reduce-scatter.2
